TPU v7x, 256 devices: a whole 4x4x8 slice. The times are simulated.
256 devices in a mesh: row: 16 (over z, core), col: 16 (over y, x).
Axes of the slice: x: 4, y: 4, z: 8, core: 2. Of those that a mesh axis runs over, the one named last changes fastest.
Arguments:
- factor: float32 [2, 16, 512, 2, 16, 512], P(None, 'row', None, None, 'col'), as said below
- pending: float32 [2, 16, 512, 16384], P(None, 'row', None, 'col'), may hold values from -0.4 to 0.4
- variance: float32 [16384], P('col'), may hold values from 2 to 4
- first_block: int32 [1], replicated, may hold values from 0 to 30
Outputs:
- pending_out: float32 [2, 16, 512, 16384], P(None, 'row', None, 'col')
- variance_out: float32 [16384], P('col')
Inputs may be any that keep to these rules, and one draw needn't show every extreme that they name: factor is lower triangular with diagonal entries from 1 to 2.
All inputs are finite; a program needn't handle non-finite values.
Results may differ from a plain program's by a relative error of at most 0.0001.
Values sent between devices are 32-bit elements; how exact they have to be, the bound alone decides.
A program may use at most 128 MiB of HBM per device.

v0:
```python
import jax
import jax.numpy as jnp
from jax import lax
from jax.sharding import PartitionSpec as P


def from_root(shard, axis, root):
    mine = lax.axis_index(axis) == root
    return lax.psum(jnp.where(mine, shard, jnp.zeros_like(shard)), axis)


def per_device(factor, pending, variance, first_block):
    row_count = lax.axis_size("row")
    col_count = lax.axis_size("col")
    row_index = lax.axis_index("row")
    cycles = factor.shape[0]
    width = factor.shape[2]
    columns = factor[:, 0, :, :, 0, :]
    current = pending[:, 0]
    blocks = jnp.arange(cycles, dtype=jnp.int32) * row_count + row_index
    first = first_block[0]
    identity = jnp.eye(width, dtype=jnp.float32)
    for offset in range(2):
        index = first + offset
        mine = lax.dynamic_index_in_dim(columns, index // col_count, axis=2, keepdims=False)
        panel_cols = from_root(mine, "col", index % col_count)
        local = index // row_count
        owner = index % row_count
        rows_now = lax.dynamic_index_in_dim(current, local, 0, keepdims=False)
        diagonal = lax.dynamic_index_in_dim(panel_cols, local, 0, keepdims=False)
        diagonal = jnp.where(row_index == owner, diagonal, identity)
        solve_solved = jax.scipy.linalg.solve_triangular(diagonal, rows_now, lower=True)
        solved = from_root(solve_solved, "row", owner)
        state = current
        product = jnp.einsum(
            "abk,kq->abq",
            panel_cols,
            solved,
            precision=lax.Precision.HIGHEST,
            preferred_element_type=jnp.float32,
        )
        state = jnp.where((blocks > index)[:, None, None], state - product, state)
        current = jnp.where((blocks == index)[:, None, None], solved[None], state)
        variance = variance - jnp.sum(solved * solved, axis=0)
    return (current[:, None], variance)


def solution(mesh):
    in_specs = (P(None, "row", None, None, "col", None), P(None, "row", None, "col"), P("col"), P())
    out_specs = (P(None, "row", None, "col"), P("col"))
    return jax.shard_map(
        per_device, mesh=mesh, in_specs=in_specs, out_specs=out_specs, check_vma=False
    )
```

profile of v0, /device:TPU:1, one launch (start us, length us, event | category | flops | bytes accessed | tf_op | source)
XLA Modules:
  0.0 460.7 jit_solution(10681021285219222026)
XLA Ops:
  7.9 5.1 %constant_dynamic-slice_fusion.3 = (f32[2,1,512,1,1,512]{5,4,3,2,1,0:T(1,128)S(1)}, f32[2,1,512,1,1,512]{5,4,3,2,1,0:T(1,128)S(1)}) fusion(f32[2,1,512,2,1,512]{5,4,3,2,1,0:T(1,128)} %param.6, s32[]{:T(128)S(6)} %select_n.104, s32[]{:T(128)S(6)} %select_n.113), kind=kLoop, calls=%fused_computation.77 | loop fusion | bytes 8388616 | tf_op jit(solution)/shard_map/jit(dynamic_index_in_dim)/dynamic_slice | solution.py:25
  13.0 2.8 fusion.3
  15.8 0.0 all-reduce.5.cloned.1.call-start
  15.9 1.7 dynamic-slice_bitcast_fusion.1
  17.7 115.7 %all-reduce.9.cloned.1.call-done = (f32[2,512,512]{2,1,0:T(8,128)}, f32[2,512,512]{2,1,0:T(8,128)}) async-done(((f32[2,512,512]{2,1,0:T(8,128)}, f32[2,512,512]{2,1,0:T(8,128)}), (f32[2,512,512]{2,1,0:T(8,128)}, f32[2,512,512]{2,1,0:T(8,128)})) %all-reduce.9.cloned.1.call-update) | async-done | bytes 4194320 | tf_op jit(solution)/shard_map/psum | solution.py:9
  133.4 1.4 fusion.26
  134.8 8.0 %while.4 = (s32[]{:T(128)}, f32[512,512]{1,0:T(8,128)S(1)}, s32[4,2]{0,1:T(2,128)S(1)}, f32[4,128,128]{2,1,0:T(8,128)S(1)}, s32[]{:T(128)}) while((s32[]{:T(128)}, f32[512,512]{1,0:T(8,128)S(1)}, s32[4,2]{0,1:T(2,128)S(1)}, f32[4,128,128]{2,1,0:T(8,128)S(1)}, s32[]{:T(128)}) %tuple.44), condition=%wide.while_cond, body=%wide.while_body.sunk | while | flops 2 | bytes 131189 | solution.py:32
  134.8 0.1 constant_dynamic-slice_fusion.6
  134.9 0.5 fusion.67
  135.4 1.4 bitcast_dynamic-update-slice_fusion.4
  136.8 0.1 constant_dynamic-slice_fusion.6
  136.9 0.5 fusion.67
  137.4 1.4 bitcast_dynamic-update-slice_fusion.4
  138.8 0.1 constant_dynamic-slice_fusion.6
  138.9 0.5 fusion.67
  139.4 1.4 bitcast_dynamic-update-slice_fusion.4
  140.8 0.1 constant_dynamic-slice_fusion.6
  140.9 0.5 fusion.67
  141.4 1.4 bitcast_dynamic-update-slice_fusion.4
  142.8 0.7 copy-done.4
  143.5 40.1 %custom-call.4 = f32[4,128,128]{1,2,0:T(8,128)S(1)} custom-call(f32[4,128,128]{2,1,0:T(8,128)} %copy-done.4), custom_call_target="InvertDiagBlocksLowerTriangular" | custom-call | tf_op jit(solution)/shard_map/jit(_solve_triangular)/triangular_solve | solution.py:32
  183.7 0.6 fusion.35
  184.3 0.6 convolution_subtract_fusion.3
  184.9 0.6 fusion.48
  185.5 0.7 convolution_subtract_fusion.1
  186.3 0.6 fusion.46
  186.9 1.1 fusion.22
  188.0 0.6 fusion.45
  188.6 1.6 maximum_select_fusion
  190.2 0.2 all-reduce.7.cloned.1.call-start
  190.4 1.3 copy-done.3
  191.8 0.1 fusion.25
  191.9 8.2 %while.5 = (s32[]{:T(128)}, f32[512,512]{1,0:T(8,128)S(1)}, s32[4,2]{0,1:T(2,128)S(1)}, f32[4,128,128]{2,1,0:T(8,128)S(1)}, s32[]{:T(128)}) while((s32[]{:T(128)}, f32[512,512]{1,0:T(8,128)S(1)}, s32[4,2]{0,1:T(2,128)S(1)}, f32[4,128,128]{2,1,0:T(8,128)S(1)}, s32[]{:T(128)}) %tuple.57), condition=%wide.while_cond.clone, body=%wide.while_body.clone.sunk | while | flops 2 | bytes 131189 | solution.py:32
  192.0 0.1 constant_dynamic-slice_fusion.7
  192.0 0.6 fusion.68
  192.6 1.4 bitcast_dynamic-update-slice_fusion.5
  194.0 0.1 constant_dynamic-slice_fusion.7
  194.1 0.6 fusion.68
  194.7 1.4 bitcast_dynamic-update-slice_fusion.5
  196.1 0.1 constant_dynamic-slice_fusion.7
  196.1 0.6 fusion.68
  196.7 1.4 bitcast_dynamic-update-slice_fusion.5
  198.1 0.1 constant_dynamic-slice_fusion.7
  198.2 0.6 fusion.68
  198.8 1.4 bitcast_dynamic-update-slice_fusion.5
  200.2 39.3 %custom-call.5 = f32[4,128,128]{1,2,0:T(8,128)S(1)} custom-call(f32[4,128,128]{2,1,0:T(8,128)S(1)} %get-tuple-element.18), custom_call_target="InvertDiagBlocksLowerTriangular" | custom-call | tf_op jit(solution)/shard_map/jit(_solve_triangular)/triangular_solve | solution.py:32
  239.5 66.1 %all-reduce.5.cloned.1.call-done = f32[512,1024]{1,0:T(8,128)} async-done(((f32[512,1024]{1,0:T(8,128)}), f32[512,1024]{1,0:T(8,128)}) %all-reduce.5.cloned.1.call-update) | async-done | bytes 2097168 | tf_op jit(solution)/shard_map/psum | solution.py:9
  305.6 11.6 %fusion = f32[2,512,1024]{2,1,0:T(8,128)S(1)} fusion(f32[2,1,512,1024]{3,2,1,0:T(8,128)} %param.7, f32[2,512,512]{2,1,0:T(8,128)} %get-tuple-element.37, f32[512,1024]{1,0:T(8,128)} %all-reduce.5.cloned.1.call-done, pred[2]{0:T(512)(128)(4,1)S(1)} %get-tuple-element.45, pred[2]{0:T(512)(128)(4,1)S(1)} %get-tuple-element.46), kind=kOutput, calls=%fused_computation.6 | convolution fusion | flops 6445596672 | bytes 12582916 | tf_op jit(solution)/shard_map/abk,kq->abq/dot_general | solution.py:35
  317.2 0.1 dynamic-slice_bitcast_fusion
  317.4 1.9 copy-done
  319.2 0.6 fusion.33
  319.9 0.6 convolution_subtract_fusion.2
  320.5 0.6 fusion.44
  321.1 0.7 convolution_subtract_fusion
  321.8 0.6 fusion.42
  322.5 1.1 fusion.19
  323.6 0.6 fusion.41
  324.2 1.6 maximum_select_fusion.1
  325.8 1.6 copy-done.1
  327.4 0.2 multiply_reduce_fusion.1
  327.6 113.4 %all-reduce.7.cloned.1.call-done = f32[512,1024]{1,0:T(8,128)} async-done(((f32[512,1024]{1,0:T(8,128)}), f32[512,1024]{1,0:T(8,128)}) %all-reduce.7.cloned.1.call-update) | async-done | bytes 2097168 | tf_op jit(solution)/shard_map/psum | solution.py:9
  441.0 1.9 multiply_reduce_fusion
  442.9 0.6 subtract_subtract_fusion
  443.5 10.7 %fusion.2 = f32[2,1,512,1024]{3,2,1,0:T(8,128)} fusion(f32[2,512,1024]{2,1,0:T(8,128)} %copy-done, f32[2,512,512]{2,1,0:T(8,128)} %get-tuple-element.38, f32[512,1024]{1,0:T(8,128)S(1)} %copy-done.2, pred[2]{0:T(512)(128)(4,1)S(1)} %get-tuple-element.47, pred[2]{0:T(512)(128)(4,1)S(1)} %get-tuple-element.48), kind=kOutput, calls=%fused_computation.8 | convolution fusion | flops 6445596672 | bytes 12582916 | tf_op jit(solution)/shard_map/abk,kq->abq/dot_general | solution.py:35
  (18 shorter events, 0.2 us)
Async XLA Ops:
  7.2 126.2 %all-reduce.9.cloned.1.call-start = ((), (), s32[]{:S(2)}) async-start(), calls=%async_computation.2 | async-start | bytes 8388608 | tf_op jit(solution)/shard_map/psum | solution.py:9
  15.8 289.7 %all-reduce.5.cloned.1.call-start = ((), (), s32[]{:S(2)}) async-start(), calls=%async_computation | async-start | bytes 4194304 | tf_op jit(solution)/shard_map/psum | solution.py:9
  142.8 0.7 copy-start.4
  190.2 1.6 copy-start.3
  190.2 250.7 %all-reduce.7.cloned.1.call-start = ((), (), s32[]{:S(2)}) async-start(), calls=%async_computation.1 | async-start | bytes 4194304 | tf_op jit(solution)/shard_map/psum | solution.py:9
  317.2 2.0 copy-start
  325.8 1.6 copy-start.1
  327.4 115.5 %copy-start.5 = (f32[1024]{0:T(1024)S(1)}, f32[1024]{0:T(1024)}, u32[]{:S(2)}) copy-start(f32[1024]{0:T(1024)} %param.8) | copy-start | bytes 12292
  441.0 2.5 copy-start.2
Sparse Core Ops, SparseCore 0:
  16.0 117.4 all-reduce.8
  190.3 115.1 all-reduce.4
  326.0 114.9 all-reduce.6
where the time goes:
time: 461 us
  waiting for transfers between devices  295 us (64%)
  other arithmetic  89.6 us (19%)
  matrix products  32.2 us (7%)
  local copies, waits for them, and re-layouts  28.5 us (6%)
  between operations  14.7 us (3%)
    psum x3, waiting for transfers between devices, from_root(): return lax.psum(jnp.where(mine, shard, jnp.zeros_like(shard)), axis)  295 us
    another operation x5, other arithmetic, per_device(): jax.scipy.linalg.solve_triangular(diagonal, rows_now, lower=True)  80.9 us
    dot_general x2, matrix products, per_device(): jnp.einsum('abk,kq->abq', panel_cols, solved, precision=lax.Precision.HIG...  22.3 us
    another operation x27, local copies, waits for them, and re-layouts, per_device(): jax.scipy.linalg.solve_triangular(diagonal, rows_now, lower=True)  16.1 us
    another operation x14, matrix products, per_device(): jax.scipy.linalg.solve_triangular(diagonal, rows_now, lower=True)  9.85 us
  transfers between devices with their start and end apart: 3, of which 3 were waited for; matrix products, arithmetic and copies ran while one was open for 11% of the time, Pallas kernels for 0%

commit v1 on v0

v1 whole, which is shorter than its diff:
```python
import functools

import jax
import jax.numpy as jnp
import numpy as np
from jax import lax
from jax.experimental import pallas as pl
from jax.experimental.pallas import tpu as pltpu
from jax.sharding import PartitionSpec as P

MESH = pl.DeviceIdType.MESH
F32 = jnp.float32
BF16 = jnp.bfloat16

PI = [
    [-1, 0, 0, 0, 1, 2, 2, 0, 1, 2, 2, 0, 1, 3, 0, 0],
    [-1, 1, 1, 1, 0, 1, 1, 2, 0, 1, 3, 2, 0, 1, 3, 3],
    [-1, 3, 3, 3, 2, 0, 0, 1, 2, 0, 1, 1, 2, 2, 2, 2],
    [-1, 2, 2, 2, 3, 3, 3, 3, 3, 3, 0, 3, 3, 0, 1, 1],
]
K = [
    [0, 1, 2, 3, 3, 2, 3, 4, 4, 3, 4, 5, 3, 2, 3, 4],
    [0, 3, 2, 1, 3, 4, 3, 2, 4, 5, 4, 3, 3, 4, 3, 2],
    [0, 3, 4, 3, 1, 2, 3, 2, 2, 3, 4, 3, 3, 4, 5, 4],
    [0, 3, 4, 3, 3, 4, 5, 4, 2, 3, 4, 3, 1, 2, 3, 2],
]
STEP = [(1, 0), (3, 0), (0, 1), (0, 3)]
DEPTH = 5
D = 4
NP = 32
SXY = NP + (DEPTH - 1) * D
SZ = NP + 7 * D
ZSEND = NP + 6 * D
EV_A2A, EV_SEL, EV_AG = 12, 20, 28
EV_STEP = 4


def hop(v, d):
    return ((v // 4 + STEP[d][1]) % 4) * 4 + (v % 4 + STEP[d][0]) % 4


def tree_table():
    rows = []
    for u in range(16):
        pick = []
        for d in range(4):
            v = hop(u, d)
            if u == 0 or v == 0:
                pick.append(4)
            else:
                c = [c for c in range(4) if PI[c][v] == d][0]
                pick.append(PI[c][u])
        rows.append(pick + [max(PI[c][u], 0) for c in range(4)] + [max(K[c][u] - 1, 0) * D for c in range(4)])
    return np.array(rows, np.int32).reshape(-1)


def iota2(n, dim):
    return lax.broadcasted_iota(jnp.int32, (n, n), dim)


def dot6(a, b):
    return jnp.dot(a, b, precision=lax.Precision.HIGHEST, preferred_element_type=F32)


def split(x):
    hi = x.astype(BF16)
    return hi, (x - hi.astype(F32)).astype(BF16)


def dot3(ah, al, bh, bl):
    f = functools.partial(jnp.dot, preferred_element_type=F32)
    return f(ah, bh) + (f(ah, bl) + f(al, bh))


def inverses(blocks):
    n = blocks[0].shape[0]
    r, c = iota2(n, 0), iota2(n, 1)
    eye = (r == c).astype(F32)
    scale = [1.0 / jnp.sum(jnp.where(r == c, b, 0.0), axis=1, keepdims=True) for b in blocks]
    scale_t = [1.0 / jnp.sum(jnp.where(r == c, b, 0.0), axis=0, keepdims=True) for b in blocks]
    strict = [jnp.where(r > c, b * s, 0.0) for b, s in zip(blocks, scale)]
    small = [jnp.where(r // 16 == c // 16, x, 0.0) for x in strict]
    inv = [eye - x for x in small]
    power = small
    for _ in range(3):
        power = [dot6(x, x) for x in power]
        inv = [dot6(e, eye + x) for e, x in zip(inv, power)]
    size = 16
    while size < n:
        off = [jnp.where((r // (2 * size) == c // (2 * size)) & (r // size != c // size), x, 0.0) for x in strict]
        mid = [dot6(f, e) for f, e in zip(off, inv)]
        inv = [e - dot6(e, m) for e, m in zip(inv, mid)]
        size *= 2
    return [e * s for e, s in zip(inv, scale_t)]


def exchange(
    first_ref, tbl_ref, f_ref, w_ref, var_ref,
    xh_ref, xl_ref, ph_ref, pl_ref, varo_ref,
    xst, xrc, zst, zrc, zpt, cand, ta, tb, tab, a2a, tg, lh, ll, dh, dl,
    xs, xr, zs, zr, zps, zpr, scs, scr, a2s, a2r, ags, agr, x2s, x2r, tps, tpr,
):
    p = lax.axis_index("row")
    s = lax.axis_index("col")
    zc, core = p // 2, lax.rem(p, 2)
    yc, xc = s // 4, lax.rem(s, 4)
    partner = (p + 1 - 2 * core, s)
    near = [
        (p, yc * 4 + lax.rem(xc + 1, 4)),
        (p, yc * 4 + lax.rem(xc + 3, 4)),
        (p, lax.rem(yc + 1, 4) * 4 + xc),
        (p, lax.rem(yc + 3, 4) * 4 + xc),
    ]
    zup = (lax.rem(zc + 1, 8) * 2 + core, s)
    zdn = (lax.rem(zc + 7, 8) * 2 + core, s)
    znear = [zup, zdn]

    def rcopy(src, dst, ssem, rsem, dev):
        return pltpu.make_async_remote_copy(
            src_ref=src, dst_ref=dst, send_sem=ssem, recv_sem=rsem, device_id=dev, device_id_type=MESH
        )

    barrier = pltpu.get_barrier_semaphore()
    for o in range(1, 16):
        pl.semaphore_signal(barrier, inc=1, device_id=(p, lax.rem(s + o, 16)), device_id_type=MESH)
        pl.semaphore_signal(barrier, inc=1, device_id=(lax.rem(p + o, 16), s), device_id_type=MESH)

    j = first_ref[0]
    j1 = j + 1
    pj, pj1 = lax.rem(j, 16), lax.rem(j1, 16)
    c1, c2 = j // 16, j1 // 16
    crit = jnp.where(p == pj1, c2, c1)
    zroot = (p == pj) | (p == pj1)
    rel = []
    for root in (pj, pj1):
        ry, rx = root // 4, lax.rem(root, 4)
        rel.append((lax.rem(yc - ry + 4, 4) * 4 + lax.rem(xc - rx + 4, 4)) * 12)
    pick = [[tbl_ref[rel[q] + d] for d in range(4)] for q in range(2)]
    where_dir = [[tbl_ref[rel[q] + 4 + c] for c in range(4)] for q in range(2)]
    where_slot = [[tbl_ref[rel[q] + 8 + c] for c in range(4)] for q in range(2)]
    proot = [rel[0] == 0, rel[1] == 0]
    cyc = [c1, c2]

    def panel(row, cyc_q, ct):
        low, high = (f_ref[pl.ds(row * 8 + c * 4 + ct, 8, stride=8), :] for c in range(2))
        return jnp.where(cyc_q == 0, low, high)

    def rhs(row):
        low, high = (w_ref[pl.ds(pl.multiple_of(a * 512 + row, 8), 8), :] for a in range(2))
        return jnp.where(crit == 0, low, high)

    is_a = s == p
    is_b = s == lax.rem(p + 15, 16)
    cidx = jnp.where(is_a, crit, c1)

    @pl.when(is_a | is_b)
    def _():
        def fill(q, _):
            for u in range(16):
                low, high = (panel(a * 512 + q * 32 + (u // 4) * 8, cidx, u % 4) for a in range(2))
                cand[q, u] = jnp.where(crit == 0, low, high)
            return 0

        lax.fori_loop(0, 16, fill, 0)

    pl.semaphore_wait(barrier, 30)

    for flag, dest, k in ((is_a, ta, 0), (is_b, tb, 1)):

        @pl.when(flag)
        def _():
            for o in range(1, 16):
                to = lax.rem(s + o, 16)
                rcopy(cand.at[to], dest, scs, scr.at[k], (p, to)).start()

    def ev_a2a():
        for flag, dest, k in ((is_a, ta, 0), (is_b, tb, 1)):

            @pl.when(flag)
            def _():
                for u in range(16):
                    dest[u] = cand[s, u]

            @pl.when(jnp.logical_not(flag))
            def _():
                rcopy(cand.at[0], dest, scs, scr.at[k], partner).wait_recv()

        for u in range(16):
            tab[u, 0] = ta[u]
            tab[u, 1] = tb[u]
        a2a[p] = tab[p]
        for o in range(1, 16):
            to = lax.rem(p + o, 16)
            rcopy(tab.at[to], a2a.at[p], a2s, a2r.at[p], (to, s)).start()

    def ev_sel():
        for o in range(1, 16):
            frm = lax.rem(p + o, 16)
            rcopy(tab.at[0], a2a.at[frm], a2s, a2r.at[frm], partner).wait_recv()
        h, u = p // 8, lax.rem(p, 8)
        tg[h, s, u, 0] = a2a[pj, 0]
        tg[h, s, u, 1] = a2a[pj1, 0]
        tg[h, s, u, 2] = a2a[pj1, 1]
        for o in range(1, 16):
            to = lax.rem(p + o, 16)
            rcopy(tg.at[h, s, u], tg.at[h, s, u], ags, agr.at[p], (to, s)).start()

    def piece(root, c):
        return tg.at[core, root, pl.ds(2 * c, 2)]

    def ev_ag(k):
        if k == 0:
            for o in range(1, 16):
                frm = lax.rem(p + o, 16)
                rcopy(
                    tg.at[0, 0, 0], tg.at[frm // 8, s, lax.rem(frm, 8)], ags, agr.at[frm], partner
                ).wait_recv()
        for w in range(16):
            for c in range(4):
                if K[c][w] != k:
                    continue
                root = lax.rem(yc + 4 - w // 4, 4) * 4 + lax.rem(xc + 4 - w % 4, 4)
                if w:
                    rcopy(piece(root, c), piece(root, c), x2s, x2r.at[root, c], partner).wait_recv()
                    rcopy(piece(root, c), piece(root, c), tps, tpr, partner).start()
                for d in range(4):
                    v = hop(w, d)
                    if v and PI[c][v] == d and (w or d == c):
                        rcopy(piece(root, c), piece(root, c), x2s, x2r.at[root, c], near[d]).start()

    def slot(t, _):
        i = jnp.minimum(t, NP - 1)
        back = t - D

        @pl.when((t >= D) & (back < SXY))
        def _():
            for d in range(4):
                rcopy(xst.at[d, back], xrc.at[d, back], xs.at[d], xr.at[d, back], near[d]).wait_recv()

        @pl.when((t >= D) & (back < ZSEND))
        def _():
            for d in range(2):
                rcopy(zst.at[d, back], zrc.at[d, back], zs.at[d], zr.at[d, back], znear[d]).wait_recv()

        @pl.when(t < D)
        def _():
            for d in range(4):
                for q in range(2):
                    for ct in range(4):
                        xst[d, t, q, :, ct * 128 : ct * 128 + 128] = panel(d * 256 + i * 8, cyc[q], ct)
            for d in range(2):
                zst[d, t] = rhs(d * 256 + i * 8)

        @pl.when((t >= D) & (t < SXY))
        def _():
            for d in range(4):
                for q in range(2):
                    for ct in range(4):
                        lanes = slice(ct * 128, ct * 128 + 128)
                        v = panel(d * 256 + i * 8, cyc[q], ct)
                        for e in range(4):
                            v = jnp.where(pick[q][d] == e, xrc[e, back, q, :, lanes], v)
                        xst[d, t, q, :, lanes] = v

        @pl.when(t >= D)
        def _():
            for d in range(2):
                zst[d, t] = jnp.where(zroot, rhs(d * 256 + i * 8), zrc[d, jnp.minimum(back, ZSEND - 1)])

        @pl.when(t < SXY)
        def _():
            for d in range(4):
                rcopy(xst.at[d, t], xrc.at[d, t], xs.at[d], xr.at[d, t], near[d]).start()

        @pl.when(t < ZSEND)
        def _():
            for d in range(2):
                rcopy(zst.at[d, t], zrc.at[d, t], zs.at[d], zr.at[d, t], znear[d]).start()

        for d in range(2):
            rcopy(zst.at[d, t], zpt.at[d, t], zps.at[d], zpr.at[d], partner).start()

        pl.when(t == EV_A2A)(ev_a2a)
        pl.when(t == EV_SEL)(ev_sel)
        for k in range(DEPTH + 1):
            pl.when(t == EV_AG + k * EV_STEP)(functools.partial(ev_ag, k))
        return 0

    lax.fori_loop(0, SZ, slot, 0)

    for d in range(4):
        rcopy(xst.at[d], xrc.at[d], xs.at[d], xr.at[d, 0], partner).wait_send()
    for d in range(2):
        rcopy(zrc.at[d], zrc.at[d], zs.at[d], zr.at[d, 0], partner).wait_send()
        rcopy(zst.at[d], zpt.at[d], zps.at[d], zpr.at[d], partner).wait()
    half = tg.at[core, pl.ds(0, 15)]
    rcopy(half, half, x2s, tpr, partner).wait_send()
    rcopy(half, half, tps, tpr, partner).wait()
    rcopy(a2a.at[pl.ds(0, 15)], a2a.at[pl.ds(0, 15)], a2s, tpr, partner).wait_send()
    rcopy(tg.at[0, pl.ds(0, 15), 0], tg.at[0, pl.ds(0, 15), 0], ags, tpr, partner).wait_send()

    @pl.when(is_a | is_b)
    def _():
        rcopy(cand.at[pl.ds(0, 15)], cand.at[pl.ds(0, 15)], scs, tpr, partner).wait_send()

    def panels(g, colour, i):
        for q in range(2):
            for ct in range(4):
                parts = []
                for e in range(2):
                    got = xrc[where_dir[q][colour], i + e + where_slot[q][colour], q, :, ct * 128 : ct * 128 + 128]
                    own = panel(g * 16 + e * 8, cyc[q], ct)
                    parts.append(jnp.where(proot[q], own, got))
                hi, lo = split(jnp.concatenate(parts, axis=0))
                lanes = slice(q * 512 + ct * 128, q * 512 + ct * 128 + 128)
                ph_ref[pl.ds(pl.multiple_of(g * 16, 16), 16), lanes] = hi
                pl_ref[pl.ds(pl.multiple_of(g * 16, 16), 16), lanes] = lo

    for colour in range(4):

        def rows(n, _):
            panels(colour * 16 + n, colour, n * 2)
            return 0

        lax.fori_loop(0, 16, rows, 0)

    def tile(b, rt, ct):
        u = (rt % 4) * 4 + ct
        return tg[u // 8, rt // 4, u % 8, b]

    def triangle(q, _):
        for b in range(3):
            for pair in range(2):
                for ct in range(4):
                    u = pair * 8 + ct
                    x = jnp.concatenate([tg[u // 8, q, u % 8, b], tg[(u + 4) // 8, q, (u + 4) % 8, b]], axis=0)
                    hi, lo = split(x)
                    rows16 = pl.ds(pl.multiple_of(q * 32 + pair * 16, 16), 16)
                    lh[b, rows16, ct * 128 : ct * 128 + 128] = hi
                    ll[b, rows16, ct * 128 : ct * 128 + 128] = lo
        return 0

    lax.fori_loop(0, 16, triangle, 0)

    def square(b, m, k):
        return jnp.concatenate(
            [
                jnp.concatenate([tile(b, m * 16 + rt, k * 1 + ct) for ct in range(1)], axis=1)
                for rt in range(16)
            ],
            axis=0,
        )

    inv = inverses([square(b, m, m) for b in range(2) for m in range(4)])
    for b in range(2):
        for m in range(2):
            top, bottom = inv[b * 4 + 2 * m], inv[b * 4 + 2 * m + 1]
            corner = -dot6(bottom, dot6(square(b, 2 * m + 1, 2 * m), top))
            for (r0, c0), x in (((0, 0), top), ((1, 1), bottom), ((1, 0), corner), ((0, 1), jnp.zeros_like(top))):
                hi, lo = split(x)
                dh[b * 2 + m, r0 * 128 : r0 * 128 + 128, c0 * 128 : c0 * 128 + 128] = hi
                dl[b * 2 + m, r0 * 128 : r0 * 128 + 128, c0 * 128 : c0 * 128 + 128] = lo

    zroots = [pj // 2, pj1 // 2]
    source = [lax.rem(pj, 2) == core, lax.rem(pj1, 2) == core]
    late = [
        [lax.rem(zc - z + 8, 8) * D for z in zroots],
        [lax.rem(z - zc + 8, 8) * D for z in zroots],
    ]

    def solve(n, _):
        lanes = pl.ds(pl.multiple_of(n * 256, 256), 256)
        squares = jnp.zeros((1, 256), F32)
        for b in range(2):
            for m in range(2):
                rows8 = []
                for i in range(32):
                    at = i + late[m][b]
                    rows8.append(jnp.where(source[b], zst[m, at, :, lanes], zpt[m, at, :, lanes]))
                r = jnp.concatenate(rows8, axis=0)
                if b == 1:
                    r = r - dot3(
                        lh[2, m * 256 : m * 256 + 256, :], ll[2, m * 256 : m * 256 + 256, :],
                        xh_ref[0:512, lanes], xl_ref[0:512, lanes],
                    )
                if m == 1:
                    r = r - dot3(
                        lh[b, 256:512, 0:256], ll[b, 256:512, 0:256],
                        xh_ref[b * 512 : b * 512 + 256, lanes], xl_ref[b * 512 : b * 512 + 256, lanes],
                    )
                rh, rl = split(r)
                x = dot3(dh[b * 2 + m], dl[b * 2 + m], rh, rl)
                hi, lo = split(x)
                at = b * 512 + m * 256
                xh_ref[at : at + 256, lanes] = hi
                xl_ref[at : at + 256, lanes] = lo
                squares = squares + jnp.sum(x * x, axis=0, keepdims=True)
        varo_ref[:, lanes] = var_ref[:, lanes] - squares
        return 0

    lax.fori_loop(0, 4, solve, 0)


def update(info_ref, ph_ref, pl_ref, xh_ref, xl_ref, w_ref, o_ref):
    n = pl.program_id(0)
    block = (n // 2) * info_ref[2] + info_ref[1]
    j = info_ref[0]

    @pl.when(block > j + 1)
    def _():
        o_ref[...] = w_ref[...] - dot3(ph_ref[...], pl_ref[...], xh_ref[...], xl_ref[...])

    @pl.when(block < j)
    def _():
        o_ref[...] = w_ref[...]

    for k in range(2):

        @pl.when(block == j + k)
        def _():
            rows = pl.ds(pl.multiple_of(k * 512 + lax.rem(n, 2) * 256, 256), 256)
            o_ref[...] = xh_ref[rows, :].astype(F32) + xl_ref[rows, :].astype(F32)


def per_device(factor, pending, variance, first_block):
    f = factor.reshape(8192, 128)
    w = pending.reshape(1024, 1024)
    vmem = pl.BlockSpec(memory_space=pltpu.VMEM)
    smem = pl.BlockSpec(memory_space=pltpu.SMEM)
    dma = pltpu.SemaphoreType.DMA
    sd = jax.ShapeDtypeStruct
    xh, xl, ph, plo, var = pl.pallas_call(
        exchange,
        out_shape=[sd((1024, 1024), BF16)] * 4 + [sd((1, 1024), F32)],
        in_specs=[smem, smem, vmem, vmem, vmem],
        out_specs=[vmem] * 5,
        scratch_shapes=[
            pltpu.VMEM((4, SXY, 2, 8, 512), F32),
            pltpu.VMEM((4, SXY, 2, 8, 512), F32),
            pltpu.VMEM((2, SZ, 8, 1024), F32),
            pltpu.VMEM((2, ZSEND, 8, 1024), F32),
            pltpu.VMEM((2, SZ, 8, 1024), F32),
            pltpu.VMEM((16, 16, 8, 128), F32),
            pltpu.VMEM((16, 8, 128), F32),
            pltpu.VMEM((16, 8, 128), F32),
            pltpu.VMEM((16, 2, 8, 128), F32),
            pltpu.VMEM((16, 2, 8, 128), F32),
            pltpu.VMEM((2, 16, 8, 3, 8, 128), F32),
            pltpu.VMEM((3, 512, 512), BF16),
            pltpu.VMEM((3, 512, 512), BF16),
            pltpu.VMEM((4, 256, 256), BF16),
            pltpu.VMEM((4, 256, 256), BF16),
            dma((4,)), dma((4, SXY)), dma((2,)), dma((2, ZSEND)), dma((2,)), dma((2,)),
            dma, dma((2,)), dma, dma((16,)), dma, dma((16,)), dma, dma((16, 4)), dma, dma,
        ],
        compiler_params=pltpu.CompilerParams(
            collective_id=0, has_side_effects=True, vmem_limit_bytes=67043328
        ),
        name="exchange",
    )(first_block, jnp.asarray(tree_table()), f, w, variance.reshape(1, 1024))

    info = jnp.stack([first_block[0], lax.axis_index("row"), jnp.int32(16)]).astype(jnp.int32)
    full = pl.BlockSpec((1024, 1024), lambda n, info: (0, 0))
    part = pl.BlockSpec((256, 1024), lambda n, info: (n, 0))
    out = pl.pallas_call(
        update,
        out_shape=sd((1024, 1024), F32),
        grid_spec=pltpu.PrefetchScalarGridSpec(
            num_scalar_prefetch=1,
            grid=(4,),
            in_specs=[part, part, full, full, part],
            out_specs=part,
        ),
        compiler_params=pltpu.CompilerParams(vmem_limit_bytes=60 << 20),
        name="update",
    )(info, ph, plo, xh, xl, w)
    return out.reshape(pending.shape), var.reshape(1024)


def solution(mesh):
    in_specs = (P(None, "row", None, None, "col", None), P(None, "row", None, "col"), P("col"), P())
    out_specs = (P(None, "row", None, "col"), P("col"))
    return jax.shard_map(
        per_device, mesh=mesh, in_specs=in_specs, out_specs=out_specs, check_vma=False
    )
```

time: 461 us -> 128 us (0.28)
  waiting for transfers between devices: 295 us -> 0 us
  Pallas kernels: 0 us -> 125 us
  other arithmetic: 89.6 us -> 0.6 us
  matrix products: 32.2 us -> 0 us
  local copies, waits for them, and re-layouts: 28.5 us -> 0.6 us
  between operations: 14.7 us -> 1.3 us
    psum x3 -> x0, waiting for transfers between devices: 295 us -> none  [from_root(): return lax.psum(jnp.where(mine, shard, jnp.zeros_like(shard)), axis)]
    pallas_call x0 -> x2, Pallas kernels: none -> 125 us  [the longest x1 114 us: per_device(): pl.pallas_call(exchange, out_shape=[sd((1024, 1024), BF16)] * 4 + [sd((1,...]
    another operation x5 -> x1, other arithmetic: 80.9 us -> 0.6 us  [per_device(): jnp.stack([first_block[0], lax.axis_index('row'), jnp.int32(16)])]
    dot_general x2 -> x0, matrix products: 22.3 us -> none  [per_device(): jnp.einsum('abk,kq->abq', panel_cols, solved, precision=lax.Precision.HIG...]
    another operation x27 -> x0, local copies, waits for them, and re-layouts: 16.1 us -> none  [per_device(): jax.scipy.linalg.solve_triangular(diagonal, rows_now, lower=True)]
    another operation x14 -> x0, matrix products: 9.85 us -> none  [per_device(): jax.scipy.linalg.solve_triangular(diagonal, rows_now, lower=True)]
    select_n x3 -> x0, other arithmetic: 5.9 us -> none  [from_root(): return lax.psum(jnp.where(mine, shard, jnp.zeros_like(shard)), axis)]
    dynamic_slice x1 -> x0, local copies, waits for them, and re-layouts: 5.1 us -> none  [per_device(): lax.dynamic_index_in_dim(columns, index // col_count, axis=2, keepdims=Fa...]
  transfers between devices with their start and end apart: 3 -> 0, of which waited for: 3 -> 0; matrix products, arithmetic and copies ran while one was open for 11% -> 0% of each run, Pallas kernels for 0% -> 0%
where the time goes in v1:
time: 128 us
  Pallas kernels  125 us (98%)
  between operations  1.3 us (1%)
    pallas_call x1, Pallas kernels, per_device(): pl.pallas_call(exchange, out_shape=[sd((1024, 1024), BF16)] * 4 + [sd((1,...  114 us
    pallas_call x1, Pallas kernels, per_device(): pl.pallas_call(update, out_shape=sd((1024, 1024), F32), grid_spec=pltpu.P...  10.9 us

profile of v1, /device:TPU:1, one launch (start us, length us, event | category | flops | bytes accessed | tf_op | source)
XLA Modules:
  0.0 127.6 jit_solution(13670465852160076403)
XLA Ops:
  1.3 0.6 pad_add_fusion.info_ref
  1.9 114.2 %exchange.1 = (bf16[1024,1024]{1,0:T(8,128)(2,1)}, bf16[1024,1024]{1,0:T(8,128)(2,1)}, bf16[1024,1024]{1,0:T(8,128)(2,1)}, bf16[1024,1024]{1,0:T(8,128)(2,1)}, f32[1,1024]{1,0:T(1,128)}) custom-call(s32[1]{0:T(128)S(6)} %copy.9.first_ref, s32[192]{0:T(256)} %constant.9.clone.tbl_ref, f32[8192,128]{1,0:T(8,128)} %bitcast.11, f32[1024,1024]{1,0:T(8,128)} %bitcast.8, ...), custom_call_target="tpu_custom_call" | custom-call | tf_op jit(solution)/shard_map/exchange/pallas_call | solution.py:432
  116.1 0.0 copy-start
  116.1 10.9 %update.1 = f32[1024,1024]{1,0:T(8,128)} custom-call(s32[3]{0:T(128)} %pad_add_fusion.info_ref, bf16[1024,1024]{1,0:T(8,128)(2,1)} %get-tuple-element.7.ph_ref, bf16[1024,1024]{1,0:T(8,128)(2,1)} %get-tuple-element.8.pl_ref, bf16[1024,1024]{1,0:T(8,128)(2,1)} %get-tuple-element.9.xh_ref, bf16[1024,1024]{1,0:T(8,128)(2,1)} %get-tuple-element.10.xl_ref, ...), custom_call_target="tpu_custom_call" | custom-call | tf_op jit(solution)/shard_map/update/pallas_call | solution.py:465
  127.0 0.0 copy-done
  127.0 0.6 copy.10
Async XLA Ops:
  116.1 10.9 %copy-start = (f32[1,1024]{1,0:T(1,128)S(1)}, f32[1,1024]{1,0:T(1,128)}, u32[]{:S(2)}) copy-start(f32[1,1024]{1,0:T(1,128)} %get-tuple-element.11) | copy-start | bytes 12292

commit v2 on v1

--- a/solution.py
+++ b/solution.py
@@ -26,13 +26,13 @@
 ]
 STEP = [(1, 0), (3, 0), (0, 1), (0, 3)]
 DEPTH = 5
-D = 4
-NP = 32
-SXY = NP + (DEPTH - 1) * D
-SZ = NP + 7 * D
-ZSEND = NP + 6 * D
-EV_A2A, EV_SEL, EV_AG = 12, 20, 28
-EV_STEP = 4
+D = 5
+DZ = 5
+NPZ = 32
+SZ = NPZ + 7 * DZ
+ZSEND = NPZ + 6 * DZ
+EV_A2A, EV_SEL, EV_AG = 16, 23, 30
+EV_STEP = 6
 
 
 def hop(v, d):
@@ -95,11 +95,16 @@
 
 
 def exchange(
-    first_ref, tbl_ref, f_ref, w_ref, var_ref,
+    base, first_ref, tbl_ref, f_ref, w_ref, var_ref,
     xh_ref, xl_ref, ph_ref, pl_ref, varo_ref,
     xst, xrc, zst, zrc, zpt, cand, ta, tb, tab, a2a, tg, lh, ll, dh, dl,
     xs, xr, zs, zr, zps, zpr, scs, scr, a2s, a2r, ags, agr, x2s, x2r, tps, tpr,
 ):
+    tall = (1024 - base) // 4
+    NPX = tall // 8
+    SXY = NPX + (DEPTH - 1) * D
+    groups = tall // 4
+    each = -(-groups // (ZSEND - SXY - D))
     p = lax.axis_index("row")
     s = lax.axis_index("col")
     zc, core = p // 2, lax.rem(p, 2)
@@ -139,15 +144,14 @@
     where_dir = [[tbl_ref[rel[q] + 4 + c] for c in range(4)] for q in range(2)]
     where_slot = [[tbl_ref[rel[q] + 8 + c] for c in range(4)] for q in range(2)]
     proot = [rel[0] == 0, rel[1] == 0]
-    cyc = [c1, c2]
+    ccyc = jnp.where(proot[0], c1, c2)
 
     def panel(row, cyc_q, ct):
         low, high = (f_ref[pl.ds(row * 8 + c * 4 + ct, 8, stride=8), :] for c in range(2))
         return jnp.where(cyc_q == 0, low, high)
 
     def rhs(row):
-        low, high = (w_ref[pl.ds(pl.multiple_of(a * 512 + row, 8), 8), :] for a in range(2))
-        return jnp.where(crit == 0, low, high)
+        return jnp.where(crit == 0, w_ref[pl.ds(row, 8), :], w_ref[pl.ds(512 + row, 8), :])
 
     is_a = s == p
     is_b = s == lax.rem(p + 15, 16)
@@ -228,57 +232,109 @@
                     if v and PI[c][v] == d and (w or d == c):
                         rcopy(piece(root, c), piece(root, c), x2s, x2r.at[root, c], near[d]).start()
 
+    def panels(g):
+        colour, i = g // (tall // 16), lax.rem(g, tall // 16) * 2
+        row = pl.multiple_of(base + g * 16, 16)
+        own = [[panel(row + e * 8, ccyc, ct) for ct in range(4)] for e in range(2)]
+        for q in range(2):
+            here, late = where_dir[q][0], where_slot[q][0]
+            for c in range(1, 4):
+                here = jnp.where(colour == c, where_dir[q][c], here)
+                late = jnp.where(colour == c, where_slot[q][c], late)
+            for ct in range(4):
+                parts = []
+                for e in range(2):
+                    got = xrc[here, i + e + late, q, :, ct * 128 : ct * 128 + 128]
+                    parts.append(jnp.where(proot[q], own[e][ct], got))
+                hi, lo = split(jnp.concatenate(parts, axis=0))
+                lanes = slice(q * 512 + ct * 128, q * 512 + ct * 128 + 128)
+                ph_ref[pl.ds(row, 16), lanes] = hi
+                pl_ref[pl.ds(row, 16), lanes] = lo
+
     def slot(t, _):
-        i = jnp.minimum(t, NP - 1)
         back = t - D
+        zback = t - DZ
+
+        own_x = base + jnp.minimum(t, NPX - 1) * 8
+        own_z = jnp.minimum(t, NPZ - 1) * 8
+
+        @pl.when(t >= DZ)
+        def _():
+            for d in range(2):
+                rcopy(zst.at[d, zback], zrc.at[d, zback], zs.at[d], zr.at[d, zback], znear[d]).wait_recv()
+
+        @pl.when(t < DZ)
+        def _():
+            for d in range(2):
+                zst[d, t] = rhs(pl.multiple_of(d * 256 + own_z, 8))
+
+        @pl.when((t >= DZ) & (t < NPZ))
+        def _():
+            for d in range(2):
+                own = rhs(pl.multiple_of(d * 256 + own_z, 8))
+                zst[d, t] = jnp.where(zroot, own, zrc[d, zback])
+
+        @pl.when(t >= NPZ)
+        def _():
+            for d in range(2):
+                zst[d, t] = zrc[d, zback]
+
+        @pl.when(t < ZSEND)
+        def _():
+            for d in range(2):
+                rcopy(zst.at[d, t], zrc.at[d, t], zs.at[d], zr.at[d, t], znear[d]).start()
+
+        for d in range(2):
+            rcopy(zst.at[d, t], zpt.at[d, t], zps.at[d], zpr.at[d], partner).start()
 
         @pl.when((t >= D) & (back < SXY))
         def _():
             for d in range(4):
                 rcopy(xst.at[d, back], xrc.at[d, back], xs.at[d], xr.at[d, back], near[d]).wait_recv()
 
-        @pl.when((t >= D) & (back < ZSEND))
-        def _():
-            for d in range(2):
-                rcopy(zst.at[d, back], zrc.at[d, back], zs.at[d], zr.at[d, back], znear[d]).wait_recv()
+        def put_xy(d):
+            rcopy(xst.at[d, t], xrc.at[d, t], xs.at[d], xr.at[d, t], near[d]).start()
 
         @pl.when(t < D)
         def _():
             for d in range(4):
-                for q in range(2):
-                    for ct in range(4):
-                        xst[d, t, q, :, ct * 128 : ct * 128 + 128] = panel(d * 256 + i * 8, cyc[q], ct)
-            for d in range(2):
-                zst[d, t] = rhs(d * 256 + i * 8)
-
-        @pl.when((t >= D) & (t < SXY))
+                for ct in range(4):
+                    lanes = slice(ct * 128, ct * 128 + 128)
+                    own = panel(d * tall + own_x, ccyc, ct)
+                    for q in range(2):
+                        xst[d, t, q, :, lanes] = own
+                put_xy(d)
+
+        @pl.when((t >= D) & (t < NPX))
         def _():
             for d in range(4):
-                for q in range(2):
-                    for ct in range(4):
-                        lanes = slice(ct * 128, ct * 128 + 128)
-                        v = panel(d * 256 + i * 8, cyc[q], ct)
+                for ct in range(4):
+                    lanes = slice(ct * 128, ct * 128 + 128)
+                    own = panel(d * tall + own_x, ccyc, ct)
+                    for q in range(2):
+                        v = own
                         for e in range(4):
                             v = jnp.where(pick[q][d] == e, xrc[e, back, q, :, lanes], v)
                         xst[d, t, q, :, lanes] = v
-
-        @pl.when(t >= D)
-        def _():
-            for d in range(2):
-                zst[d, t] = jnp.where(zroot, rhs(d * 256 + i * 8), zrc[d, jnp.minimum(back, ZSEND - 1)])
-
-        @pl.when(t < SXY)
+                put_xy(d)
+
+        @pl.when((t >= NPX) & (t < SXY))
         def _():
             for d in range(4):
-                rcopy(xst.at[d, t], xrc.at[d, t], xs.at[d], xr.at[d, t], near[d]).start()
-
-        @pl.when(t < ZSEND)
-        def _():
-            for d in range(2):
-                rcopy(zst.at[d, t], zrc.at[d, t], zs.at[d], zr.at[d, t], znear[d]).start()
-
-        for d in range(2):
-            rcopy(zst.at[d, t], zpt.at[d, t], zps.at[d], zpr.at[d], partner).start()
+                for q in range(2):
+                    v = xrc[0, back, q]
+                    for e in range(1, 4):
+                        v = jnp.where(pick[q][d] == e, xrc[e, back, q], v)
+                    xst[d, t, q] = v
+                put_xy(d)
+
+        @pl.when((t >= SXY + D) & (t < ZSEND))
+        def _():
+            def rows(n, _):
+                panels(jnp.minimum((t - SXY - D) * each + n, groups - 1))
+                return 0
+
+            lax.fori_loop(0, each, rows, 0)
 
         pl.when(t == EV_A2A)(ev_a2a)
         pl.when(t == EV_SEL)(ev_sel)
@@ -286,43 +342,10 @@
             pl.when(t == EV_AG + k * EV_STEP)(functools.partial(ev_ag, k))
         return 0
 
-    lax.fori_loop(0, SZ, slot, 0)
-
-    for d in range(4):
-        rcopy(xst.at[d], xrc.at[d], xs.at[d], xr.at[d, 0], partner).wait_send()
-    for d in range(2):
-        rcopy(zrc.at[d], zrc.at[d], zs.at[d], zr.at[d, 0], partner).wait_send()
-        rcopy(zst.at[d], zpt.at[d], zps.at[d], zpr.at[d], partner).wait()
+    lax.fori_loop(0, ZSEND, slot, 0)
+
     half = tg.at[core, pl.ds(0, 15)]
-    rcopy(half, half, x2s, tpr, partner).wait_send()
     rcopy(half, half, tps, tpr, partner).wait()
-    rcopy(a2a.at[pl.ds(0, 15)], a2a.at[pl.ds(0, 15)], a2s, tpr, partner).wait_send()
-    rcopy(tg.at[0, pl.ds(0, 15), 0], tg.at[0, pl.ds(0, 15), 0], ags, tpr, partner).wait_send()
-
-    @pl.when(is_a | is_b)
-    def _():
-        rcopy(cand.at[pl.ds(0, 15)], cand.at[pl.ds(0, 15)], scs, tpr, partner).wait_send()
-
-    def panels(g, colour, i):
-        for q in range(2):
-            for ct in range(4):
-                parts = []
-                for e in range(2):
-                    got = xrc[where_dir[q][colour], i + e + where_slot[q][colour], q, :, ct * 128 : ct * 128 + 128]
-                    own = panel(g * 16 + e * 8, cyc[q], ct)
-                    parts.append(jnp.where(proot[q], own, got))
-                hi, lo = split(jnp.concatenate(parts, axis=0))
-                lanes = slice(q * 512 + ct * 128, q * 512 + ct * 128 + 128)
-                ph_ref[pl.ds(pl.multiple_of(g * 16, 16), 16), lanes] = hi
-                pl_ref[pl.ds(pl.multiple_of(g * 16, 16), 16), lanes] = lo
-
-    for colour in range(4):
-
-        def rows(n, _):
-            panels(colour * 16 + n, colour, n * 2)
-            return 0
-
-        lax.fori_loop(0, 16, rows, 0)
 
     def tile(b, rt, ct):
         u = (rt % 4) * 4 + ct
@@ -361,11 +384,26 @@
                 dh[b * 2 + m, r0 * 128 : r0 * 128 + 128, c0 * 128 : c0 * 128 + 128] = hi
                 dl[b * 2 + m, r0 * 128 : r0 * 128 + 128, c0 * 128 : c0 * 128 + 128] = lo
 
+    lax.fori_loop(ZSEND, SZ, slot, 0)
+
+    for d in range(4):
+        rcopy(xst.at[d], xrc.at[d], xs.at[d], xr.at[d, 0], partner).wait_send()
+    for d in range(2):
+        rcopy(zrc.at[d], zrc.at[d], zs.at[d], zr.at[d, 0], partner).wait_send()
+        rcopy(zst.at[d], zpt.at[d], zps.at[d], zpr.at[d], partner).wait()
+    rcopy(half, half, x2s, tpr, partner).wait_send()
+    rcopy(a2a.at[pl.ds(0, 15)], a2a.at[pl.ds(0, 15)], a2s, tpr, partner).wait_send()
+    rcopy(tg.at[0, pl.ds(0, 15), 0], tg.at[0, pl.ds(0, 15), 0], ags, tpr, partner).wait_send()
+
+    @pl.when(is_a | is_b)
+    def _():
+        rcopy(cand.at[pl.ds(0, 15)], cand.at[pl.ds(0, 15)], scs, tpr, partner).wait_send()
+
     zroots = [pj // 2, pj1 // 2]
     source = [lax.rem(pj, 2) == core, lax.rem(pj1, 2) == core]
     late = [
-        [lax.rem(zc - z + 8, 8) * D for z in zroots],
-        [lax.rem(z - zc + 8, 8) * D for z in zroots],
+        [lax.rem(zc - z + 8, 8) * DZ for z in zroots],
+        [lax.rem(z - zc + 8, 8) * DZ for z in zroots],
     ]
 
     def solve(n, _):
@@ -429,35 +467,44 @@
     smem = pl.BlockSpec(memory_space=pltpu.SMEM)
     dma = pltpu.SemaphoreType.DMA
     sd = jax.ShapeDtypeStruct
-    xh, xl, ph, plo, var = pl.pallas_call(
-        exchange,
-        out_shape=[sd((1024, 1024), BF16)] * 4 + [sd((1, 1024), F32)],
-        in_specs=[smem, smem, vmem, vmem, vmem],
-        out_specs=[vmem] * 5,
-        scratch_shapes=[
-            pltpu.VMEM((4, SXY, 2, 8, 512), F32),
-            pltpu.VMEM((4, SXY, 2, 8, 512), F32),
-            pltpu.VMEM((2, SZ, 8, 1024), F32),
-            pltpu.VMEM((2, ZSEND, 8, 1024), F32),
-            pltpu.VMEM((2, SZ, 8, 1024), F32),
-            pltpu.VMEM((16, 16, 8, 128), F32),
-            pltpu.VMEM((16, 8, 128), F32),
-            pltpu.VMEM((16, 8, 128), F32),
-            pltpu.VMEM((16, 2, 8, 128), F32),
-            pltpu.VMEM((16, 2, 8, 128), F32),
-            pltpu.VMEM((2, 16, 8, 3, 8, 128), F32),
-            pltpu.VMEM((3, 512, 512), BF16),
-            pltpu.VMEM((3, 512, 512), BF16),
-            pltpu.VMEM((4, 256, 256), BF16),
-            pltpu.VMEM((4, 256, 256), BF16),
-            dma((4,)), dma((4, SXY)), dma((2,)), dma((2, ZSEND)), dma((2,)), dma((2,)),
-            dma, dma((2,)), dma, dma((16,)), dma, dma((16,)), dma, dma((16, 4)), dma, dma,
-        ],
-        compiler_params=pltpu.CompilerParams(
-            collective_id=0, has_side_effects=True, vmem_limit_bytes=67043328
-        ),
-        name="exchange",
-    )(first_block, jnp.asarray(tree_table()), f, w, variance.reshape(1, 1024))
+    def moved(base, *operands):
+        sxy = (1024 - base) // 32 + (DEPTH - 1) * D
+        return pl.pallas_call(
+            functools.partial(exchange, base),
+            out_shape=[sd((1024, 1024), BF16)] * 4 + [sd((1, 1024), F32)],
+            in_specs=[smem, smem, vmem, vmem, vmem],
+            out_specs=[vmem] * 5,
+            scratch_shapes=[
+                pltpu.VMEM((4, sxy, 2, 8, 512), F32),
+                pltpu.VMEM((4, sxy, 2, 8, 512), F32),
+                pltpu.VMEM((2, SZ, 8, 1024), F32),
+                pltpu.VMEM((2, ZSEND, 8, 1024), F32),
+                pltpu.VMEM((2, SZ, 8, 1024), F32),
+                pltpu.VMEM((16, 16, 8, 128), F32),
+                pltpu.VMEM((16, 8, 128), F32),
+                pltpu.VMEM((16, 8, 128), F32),
+                pltpu.VMEM((16, 2, 8, 128), F32),
+                pltpu.VMEM((16, 2, 8, 128), F32),
+                pltpu.VMEM((2, 16, 8, 3, 8, 128), F32),
+                pltpu.VMEM((3, 512, 512), BF16),
+                pltpu.VMEM((3, 512, 512), BF16),
+                pltpu.VMEM((4, 256, 256), BF16),
+                pltpu.VMEM((4, 256, 256), BF16),
+                dma((4,)), dma((4, sxy)), dma((2,)), dma((2, ZSEND)), dma((2,)), dma((2,)),
+                dma, dma((2,)), dma, dma((16,)), dma, dma((16,)), dma, dma((16, 4)), dma, dma,
+            ],
+            compiler_params=pltpu.CompilerParams(
+                collective_id=base // 512, has_side_effects=True, vmem_limit_bytes=67043328
+            ),
+            name="exchange" + str(base),
+        )(*operands)
+
+    xh, xl, ph, plo, var = lax.cond(
+        first_block[0] >= 15,
+        functools.partial(moved, 512),
+        functools.partial(moved, 0),
+        first_block, jnp.asarray(tree_table()), f, w, variance.reshape(1, 1024),
+    )
 
     info = jnp.stack([first_block[0], lax.axis_index("row"), jnp.int32(16)]).astype(jnp.int32)
     full = pl.BlockSpec((1024, 1024), lambda n, info: (0, 0))

time: 128 us -> 122 us (0.953)
  Pallas kernels: 125 us -> 119 us
    pallas_call x1, Pallas kernels: 114 us -> 108 us  [moved(): pl.pallas_call(functools.partial(exchange, base), out_shape=[sd((1024, 10...]
where the time goes in v2:
time: 122 us
  Pallas kernels  119 us (98%)
  between operations  1.3 us (1%)
    pallas_call x1, Pallas kernels, moved(): pl.pallas_call(functools.partial(exchange, base), out_shape=[sd((1024, 10...  108 us
    pallas_call x1, Pallas kernels, per_device(): pl.pallas_call(update, out_shape=sd((1024, 1024), F32), grid_spec=pltpu.P...  10.9 us

profile of v2, /device:TPU:1, one launch (start us, length us, event | category | flops | bytes accessed | tf_op | source)
XLA Modules:
  0.0 121.6 jit_solution(2973445321138773831)
XLA Ops:
  1.3 0.6 pad_add_fusion.info_ref
  1.9 108.2 %conditional.1 = ((bf16[1024,1024]{1,0:T(8,128)(2,1)}, bf16[1024,1024]{1,0:T(8,128)(2,1)}, bf16[1024,1024]{1,0:T(8,128)(2,1)}, bf16[1024,1024]{1,0:T(8,128)(2,1)}, f32[1,1024]{1,0:T(1,128)})) conditional(s32[]{:T(128)} %bitcast.1, (s32[1]{0:T(128)}, f32[2,1,512,2,1,512]{5,4,3,2,1,0:T(1,128)}, f32[1024,1024]{1,0:T(8,128)}, ...), branch_computations={%region_0.0_spmd.clone, %region_1.0_spmd.clone} | conditional | bytes 8 | solution.py:502
  1.9 108.0 %exchange0.1 = (bf16[1024,1024]{1,0:T(8,128)(2,1)}, bf16[1024,1024]{1,0:T(8,128)(2,1)}, bf16[1024,1024]{1,0:T(8,128)(2,1)}, bf16[1024,1024]{1,0:T(8,128)(2,1)}, f32[1,1024]{1,0:T(1,128)}) custom-call(s32[1]{0:T(128)} %get-tuple-element.86.first_ref, s32[192]{0:T(256)} %constant.12.clone.3.tbl_ref, f32[8192,128]{1,0:T(8,128)} %bitcast.14, ...), custom_call_target="tpu_custom_call" | custom-call | tf_op jit(solution)/shard_map/cond/branch_0_fun/exchange0/pallas_call | solution.py:472
  110.1 0.0 copy-start
  110.1 10.9 %update.1 = f32[1024,1024]{1,0:T(8,128)} custom-call(s32[3]{0:T(128)} %pad_add_fusion.info_ref, bf16[1024,1024]{1,0:T(8,128)(2,1)} %get-tuple-element.125.ph_ref, bf16[1024,1024]{1,0:T(8,128)(2,1)} %get-tuple-element.124.pl_ref, bf16[1024,1024]{1,0:T(8,128)(2,1)} %get-tuple-element.127.xh_ref, bf16[1024,1024]{1,0:T(8,128)(2,1)} %get-tuple-element.126.xl_ref, ...), custom_call_target="tpu_custom_call" | custom-call | tf_op jit(solution)/shard_map/update/pallas_call | solution.py:512
  121.0 0.0 copy-done
  121.0 0.6 copy.34
Async XLA Ops:
  110.1 10.9 %copy-start = (f32[1,1024]{1,0:T(1,128)S(1)}, f32[1,1024]{1,0:T(1,128)}, u32[]{:S(2)}) copy-start(f32[1,1024]{1,0:T(1,128)} %get-tuple-element.123) | copy-start | bytes 12292

commit v3 on v2

--- a/solution.py
+++ b/solution.py
@@ -446,7 +446,8 @@
 
     @pl.when(block > j + 1)
     def _():
-        o_ref[...] = w_ref[...] - dot3(ph_ref[...], pl_ref[...], xh_ref[...], xl_ref[...])
+        here = pl.ds(pl.multiple_of(n * 256, 256), 256)
+        o_ref[...] = w_ref[...] - dot3(ph_ref[here, :], pl_ref[here, :], xh_ref[...], xl_ref[...])
 
     @pl.when(block < j)
     def _():
@@ -471,7 +472,7 @@
         sxy = (1024 - base) // 32 + (DEPTH - 1) * D
         return pl.pallas_call(
             functools.partial(exchange, base),
-            out_shape=[sd((1024, 1024), BF16)] * 4 + [sd((1, 1024), F32)],
+            out_shape=[pltpu.VMEM((1024, 1024), BF16)] * 4 + [sd((1, 1024), F32)],
             in_specs=[smem, smem, vmem, vmem, vmem],
             out_specs=[vmem] * 5,
             scratch_shapes=[
@@ -494,7 +495,7 @@
                 dma, dma((2,)), dma, dma((16,)), dma, dma((16,)), dma, dma((16, 4)), dma, dma,
             ],
             compiler_params=pltpu.CompilerParams(
-                collective_id=base // 512, has_side_effects=True, vmem_limit_bytes=67043328
+                collective_id=base // 512, has_side_effects=True, vmem_limit_bytes=48 << 20
             ),
             name="exchange" + str(base),
         )(*operands)
@@ -507,7 +508,7 @@
     )
 
     info = jnp.stack([first_block[0], lax.axis_index("row"), jnp.int32(16)]).astype(jnp.int32)
-    full = pl.BlockSpec((1024, 1024), lambda n, info: (0, 0))
+    full = pl.BlockSpec(memory_space=pltpu.VMEM)
     part = pl.BlockSpec((256, 1024), lambda n, info: (n, 0))
     out = pl.pallas_call(
         update,
@@ -515,10 +516,10 @@
         grid_spec=pltpu.PrefetchScalarGridSpec(
             num_scalar_prefetch=1,
             grid=(4,),
-            in_specs=[part, part, full, full, part],
+            in_specs=[full] * 4 + [part],
             out_specs=part,
         ),
-        compiler_params=pltpu.CompilerParams(vmem_limit_bytes=60 << 20),
+        compiler_params=pltpu.CompilerParams(vmem_limit_bytes=14 << 20),
         name="update",
     )(info, ph, plo, xh, xl, w)
     return out.reshape(pending.shape), var.reshape(1024)

time: 122 us -> 107 us (0.88)
  Pallas kernels: 119 us -> 105 us
    pallas_call x1, Pallas kernels: 108 us -> 99.6 us  [moved(): pl.pallas_call(functools.partial(exchange, base), out_shape=[pltpu.VMEM((...]
    pallas_call x1, Pallas kernels: 10.9 us -> 5.31 us  [per_device(): pl.pallas_call(update, out_shape=sd((1024, 1024), F32), grid_spec=pltpu.P...]
where the time goes in v3:
time: 107 us
  Pallas kernels  105 us (98%)
  between operations  1.29 us (1%)
    pallas_call x1, Pallas kernels, moved(): pl.pallas_call(functools.partial(exchange, base), out_shape=[pltpu.VMEM((...  99.6 us
    pallas_call x1, Pallas kernels, per_device(): pl.pallas_call(update, out_shape=sd((1024, 1024), F32), grid_spec=pltpu.P...  5.31 us

profile of v3, /device:TPU:1, one launch (start us, length us, event | category | flops | bytes accessed | tf_op | source)
XLA Modules:
  0.0 107.0 jit_solution(5779047232512981575)
XLA Ops:
  1.3 0.1 pad_add_fusion.info_ref
  1.4 99.7 %conditional.1 = ((bf16[1024,1024]{1,0:T(8,128)(2,1)S(1)}, bf16[1024,1024]{1,0:T(8,128)(2,1)S(1)}, bf16[1024,1024]{1,0:T(8,128)(2,1)S(1)}, bf16[1024,1024]{1,0:T(8,128)(2,1)S(1)}, f32[1,1024]{1,0:T(1,128)S(1)})) conditional(s32[]{:T(128)} %bitcast.1, (s32[1]{0:T(128)}, f32[2,1,512,2,1,512]{5,4,3,2,1,0:T(1,128)}, f32[1024,1024]{1,0:T(8,128)}, ...), branch_computations={%region_0.0_spmd.clone, %region_1.0_spmd.clone} | conditional | bytes 8 | solution.py:503
  1.5 99.6 %exchange512.1 = (bf16[1024,1024]{1,0:T(8,128)(2,1)S(1)}, bf16[1024,1024]{1,0:T(8,128)(2,1)S(1)}, bf16[1024,1024]{1,0:T(8,128)(2,1)S(1)}, bf16[1024,1024]{1,0:T(8,128)(2,1)S(1)}, f32[1,1024]{1,0:T(1,128)S(1)}) custom-call(s32[1]{0:T(128)} %get-tuple-element.99.first_ref, s32[192]{0:T(256)} %constant.12.clone.4.tbl_ref, f32[8192,128]{1,0:T(8,128)} %bitcast.15, ...), custom_call_target="tpu_custom_call" | custom-call | tf_op jit(solution)/shard_map/cond/branch_1_fun/exchange512/pallas_call | solution.py:473
  101.1 5.3 %update.1 = f32[1024,1024]{1,0:T(8,128)} custom-call(s32[3]{0:T(128)S(1)} %pad_add_fusion.info_ref, bf16[1024,1024]{1,0:T(8,128)(2,1)S(1)} %get-tuple-element.125.ph_ref, bf16[1024,1024]{1,0:T(8,128)(2,1)S(1)} %get-tuple-element.124.pl_ref, bf16[1024,1024]{1,0:T(8,128)(2,1)S(1)} %get-tuple-element.127.xh_ref, ...), custom_call_target="tpu_custom_call" | custom-call | tf_op jit(solution)/shard_map/update/pallas_call | solution.py:513
  106.4 0.6 copy.34
